TPU v7x, 32 devices: a whole 2x2x4 slice. The times are simulated.
32 devices in a mesh: dp: 8 (over y, x, core), ctx: 4 (over z).
Axes of the slice: x: 2, y: 2, z: 4, core: 2. Of those that a mesh axis runs over, the one named last changes fastest.
Arguments:
- queries: bfloat16 [16384, 512], P(('dp', 'ctx')), parts along dimension 0, may hold values from -60 to 60
- key_vectors: bfloat16 [16384, 128], P(('dp', 'ctx')), parts along dimension 0, may hold values from -20 to 20
- value_vectors: bfloat16 [16384, 128], P(('dp', 'ctx')), parts along dimension 0, may hold values from -6 to 6
- block_plan: int32 [64], P('dp'), parts along dimension 0, may hold values from 0 to 7, each once
- doc_lengths: int32 [64], P('dp'), parts along dimension 0, may hold values from 1 to 1024, 2048 in all
- out_weight: bfloat16 [512, 4096], P(None, 'ctx'), may hold values from -0.25 to 0.25
Outputs:
- output: bfloat16 [16384, 4096], P(('dp', 'ctx')), parts along dimension 0
There are 8 independent parts, one for each index of `dp`. A program takes and returns all parts, laid end to end along the dimension named above; an argument that names none is the same for every part. Nothing has to cross between parts.
Inputs may be any that keep to these rules, and one draw needn't show every extreme that they name: `doc_lengths`: the 8 lengths sum to 2048.
All inputs are finite; a program needn't handle non-finite values.
Results may differ from a plain program's by a relative error of at most 0.013.
Values may be sent and summed in bfloat16 or wider, within the bound.
No kernel may reach another device: no remote copies, remote signals or barrier semaphores. Data moves between devices by JAX's collectives and lax.ppermute only.
A program may use at most 64 MiB of HBM per device.

v0:
```python
import math
import jax
import jax.numpy as jnp
from jax import lax
from jax.sharding import PartitionSpec as P


def positions(block_plan, first_row, row_count, half_rows):
    row_ids = first_row + jnp.arange(row_count, dtype=jnp.int32)
    block_ids = row_ids // half_rows
    block_table = jnp.arange(block_plan.shape[0], dtype=jnp.int32)
    block_start = jnp.sum(
        jnp.where(block_ids[:, None] == block_table[None, :], block_plan[None, :], 0), axis=1
    )
    return block_start * half_rows + row_ids % half_rows


def document_ids(position, doc_ends):
    return jnp.sum((position[:, None] >= doc_ends[None, :]).astype(jnp.int32), axis=1)


def update(state, query_rows, allowed, key_block, value_block, score_scale):
    row_max, row_total, weighted = state
    scores = (
        jnp.einsum("rgd,kd->grk", query_rows, key_block, preferred_element_type=jnp.float32)
        * score_scale
    )
    scores = jnp.where(allowed[None], scores, jnp.float32(-1e30))
    new_max = jnp.maximum(row_max, jnp.max(scores, axis=2))
    weights = jnp.where(allowed[None], jnp.exp(scores - new_max[:, :, None]), jnp.float32(0.0))
    rescale = jnp.exp(row_max - new_max)
    new_total = row_total * rescale + jnp.sum(weights, axis=2)
    probs = weights.astype(jnp.bfloat16)
    new_weighted = weighted * jnp.transpose(rescale)[:, :, None] + jnp.einsum(
        "grk,kd->rgd", probs, value_block, preferred_element_type=jnp.float32
    )
    return (new_max, new_total, new_weighted)


def shards(queries, key_vectors, value_vectors, block_plan, doc_lengths, out_weight):
    span_rows = queries.shape[0]
    half_rows = span_rows // 2
    head_width = key_vectors.shape[1]
    head_count = queries.shape[1] // head_width
    score_scale = 1.0 / math.sqrt(head_width)
    first_row = lax.axis_index("ctx") * span_rows
    doc_ends = jnp.cumsum(doc_lengths)
    query_pos = positions(block_plan, first_row, span_rows, half_rows)
    query_doc = document_ids(query_pos, doc_ends)
    query_heads = queries.reshape(span_rows, head_count, head_width)
    initial = (
        jnp.full((head_count, span_rows), -1e30, jnp.float32),
        jnp.zeros((head_count, span_rows), jnp.float32),
        jnp.zeros((span_rows, head_count, head_width), jnp.float32),
    )
    key_piece = lax.all_gather(key_vectors, "ctx", axis=0, tiled=True)
    value_piece = lax.all_gather(value_vectors, "ctx", axis=0, tiled=True)
    piece_rows = key_piece.shape[0]
    block_rows = math.gcd(piece_rows, span_rows)

    def one_block(block_index, inner):
        offset = block_index * block_rows
        key_block = lax.dynamic_slice_in_dim(key_piece, offset, block_rows, 0)
        value_block = lax.dynamic_slice_in_dim(value_piece, offset, block_rows, 0)
        key_pos = positions(block_plan, offset, block_rows, half_rows)
        key_doc = document_ids(key_pos, doc_ends)
        allowed = (key_pos[None, :] <= query_pos[:, None]) & (
            key_doc[None, :] == query_doc[:, None]
        )
        results = []
        for half_index in range(2):
            low = half_index * half_rows
            high = low + half_rows
            sub_state = (inner[0][:, low:high], inner[1][:, low:high], inner[2][low:high])
            sub_mask = allowed[low:high]
            sub_query = query_heads[low:high]

            def compute(given, sub_query=sub_query, sub_mask=sub_mask):
                return update(given, sub_query, sub_mask, key_block, value_block, score_scale)

            def keep_state(given):
                return given

            results.append(lax.cond(jnp.any(sub_mask), compute, keep_state, sub_state))
        return (
            jnp.concatenate([results[0][0], results[1][0]], axis=1),
            jnp.concatenate([results[0][1], results[1][1]], axis=1),
            jnp.concatenate([results[0][2], results[1][2]], axis=0),
        )

    row_max, row_total, weighted = lax.fori_loop(0, piece_rows // block_rows, one_block, initial)
    attended = (
        (weighted / jnp.transpose(row_total)[:, :, None])
        .reshape(span_rows, head_count * head_width)
        .astype(jnp.bfloat16)
    )
    return jnp.dot(
        attended,
        lax.all_gather(out_weight, "ctx", axis=1, tiled=True),
        preferred_element_type=jnp.float32,
    ).astype(jnp.bfloat16)


def solution(mesh):
    placed = (
        P(("dp", "ctx"), None),
        P(("dp", "ctx"), None),
        P(("dp", "ctx"), None),
        P("dp"),
        P("dp"),
        P(None, "ctx"),
    )
    return jax.shard_map(
        shards, mesh=mesh, in_specs=placed, out_specs=P(("dp", "ctx"), None), check_vma=False
    )
```

profile of v0, /device:TPU:0, one launch (start us, length us, event | category | flops | bytes accessed | tf_op | source)
XLA Modules:
  0.0 117.2 jit_solution(8152489457986995129)
XLA Ops:
  6.5 0.7 all-gather.2.cloned.1.call-update
  7.3 0.7 select_reduce_fusion.1
  8.0 0.8 reduce-window.8
  8.9 1.3 %copy.16 = bf16[512,512]{0,1:T(8,128)(2,1)S(1)} copy(bf16[512,512]{1,0:T(8,128)(2,1)} %param.12) | data formatting | bytes 1048576 | tf_op args[0]
  10.4 22.6 %all_gather.10 = bf16[2048,128]{1,0:T(8,128)(2,1)} all-gather(bf16[512,128]{1,0:T(8,128)(2,1)S(1)} %copy-done), channel_id=1, replica_groups=mesh['dp'=8,'ctx'=4] {'ctx'}, dimensions={0}, use_global_device_ids=true | all-gather | bytes 655360 | tf_op jit(solution)/shard_map/all_gather | solution.py:57
  33.0 22.3 %all_gather.9 = bf16[2048,128]{1,0:T(8,128)(2,1)} all-gather(bf16[512,128]{1,0:T(8,128)(2,1)S(1)} %copy-done.1), channel_id=1, replica_groups=mesh['dp'=8,'ctx'=4] {'ctx'}, dimensions={0}, use_global_device_ids=true | all-gather | bytes 655360 | tf_op jit(solution)/shard_map/all_gather | solution.py:56
  55.4 21.3 %while.19 = (s32[]{:T(128)}, f32[4,512]{1,0:T(4,128)S(1)}, f32[4,512]{1,0:T(4,128)S(1)}, f32[512,4,128]{2,0,1:T(8,128)S(1)}, s32[8]{0:T(128)S(1)}, /*index=5*/s3...) while((s32[]{:T(128)}, f32[4,512]{1,0:T(4,128)S(1)}, ...), condition=%wide.region_16.17_spmd, body=%wide.region_3.16_spmd.sunk | while | flops 552386560 | bytes 22239732 | solution.py:91
  55.9 0.9 slice_reduce_fusion.3
  56.8 1.0 constant_dynamic-slice_fusion.3
  58.5 1.9 %conditional.5 = ((f32[4,256]{1,0:T(4,128)S(1)}, f32[4,256]{1,0:T(4,128)S(1)}, f32[256,4,128]{2,0,1:T(8,128)S(1)})) conditional(s32[]{:T(128)} %convert_element_type.65, (f32[4,256]{1,0:T(4,128)S(1)}, f32[4,256]{1,0:T(4,128)S(1)}, f32[256,4,128]{2,0,1:T(8,128)S(1)}) %tuple.79, (pred[256,512]{0,1:T(8,128)(4,1)S(1)}, ...), branch_computations={%region_7.7_spmd, %region_8.10_spmd} | conditional | flops 275516416 | bytes 8323104 | solution.py:84
  58.6 0.5 fusion
  59.1 0.9 fusion.3
  59.9 0.5 fusion.2
  61.1 1.9 %conditional.4 = ((f32[4,256]{1,0:T(4,128)S(1)}, f32[4,256]{1,0:T(4,128)S(1)}, f32[256,4,128]{2,0,1:T(8,128)S(1)})) conditional(s32[]{:T(128)} %convert_element_type.64, (f32[4,256]{1,0:T(4,128)S(1)}, f32[4,256]{1,0:T(4,128)S(1)}, f32[256,4,128]{2,0,1:T(8,128)S(1)}) %tuple.77, (pred[256,512]{0,1:T(8,128)(4,1)S(1)}, ...), branch_computations={%region_12.12_spmd, %region_13.15_spmd} | conditional | flops 275516416 | bytes 8323104 | solution.py:84
  61.1 0.5 fusion.17
  61.6 0.9 fusion.20
  62.5 0.5 fusion.19
  63.4 0.3 compare_and_fusion.2
  63.7 0.9 slice_reduce_fusion.3
  64.6 1.0 constant_dynamic-slice_fusion.3
  67.3 0.3 compare_and_fusion.2
  67.6 0.9 slice_reduce_fusion.3
  68.4 1.0 constant_dynamic-slice_fusion.3
  70.8 1.9 %conditional.4 = ((f32[4,256]{1,0:T(4,128)S(1)}, f32[4,256]{1,0:T(4,128)S(1)}, f32[256,4,128]{2,0,1:T(8,128)S(1)})) conditional(s32[]{:T(128)} %convert_element_type.64, (f32[4,256]{1,0:T(4,128)S(1)}, f32[4,256]{1,0:T(4,128)S(1)}, f32[256,4,128]{2,0,1:T(8,128)S(1)}) %tuple.77, (pred[256,512]{0,1:T(8,128)(4,1)S(1)}, ...), branch_computations={%region_12.12_spmd, %region_13.15_spmd} | conditional | flops 275516416 | bytes 8323104 | solution.py:84
  70.8 0.5 fusion.17
  71.3 0.9 fusion.20
  72.2 0.5 fusion.19
  73.4 0.9 slice_reduce_fusion.3
  74.2 1.0 constant_dynamic-slice_fusion.3
  76.7 0.3 copy.18
  77.2 26.6 %all-gather.2.cloned.1.call-done = bf16[512,4096]{1,0:T(8,128)(2,1)} async-done(((bf16[512,1024]{1,0:T(8,128)(2,1)}), bf16[512,4096]{1,0:T(8,128)(2,1)}) %all-gather.2.cloned.1.call-update) | async-done | bytes 4194320 | tf_op jit(solution)/shard_map/all_gather | solution.py:99
  103.8 6.6 %convolution_convert_fusion = bf16[512,4096]{1,0:T(8,128)(2,1)} fusion(bf16[512,512]{0,1:T(8,128)(2,1)S(1)} %bitcast.57, bf16[512,4096]{1,0:T(8,128)(2,1)} %all-gather.2.cloned.1.call-done), kind=kOutput, calls=%fused_computation.64 | convolution fusion | flops 2149580800 | bytes 8912896 | tf_op jit(solution)/shard_map/dot_general | solution.py:97
  (67 shorter events, 2.7 us)
Async XLA Ops:
  6.5 3.9 %copy-start = (bf16[512,128]{1,0:T(8,128)(2,1)S(1)}, bf16[512,128]{1,0:T(8,128)(2,1)}, u32[]{:S(2)}) copy-start(bf16[512,128]{1,0:T(8,128)(2,1)} %param.14) | copy-start | bytes 393220
  6.5 26.5 %copy-start.1 = (bf16[512,128]{1,0:T(8,128)(2,1)S(1)}, bf16[512,128]{1,0:T(8,128)(2,1)}, u32[]{:S(2)}) copy-start(bf16[512,128]{1,0:T(8,128)(2,1)} %param.13) | copy-start | bytes 393220
  6.5 97.3 %all-gather.2.cloned.1.call-start = ((), (), s32[]{:S(2)}) async-start(), calls=%async_computation | async-start | bytes 5242880 | tf_op jit(solution)/shard_map/all_gather | solution.py:99
  8.9 46.6 %copy-start.2 = (s32[8]{0:T(128)S(1)}, s32[8]{0:T(128)}, u32[]{:S(2)}) copy-start(s32[8]{0:T(128)} %param.15) | copy-start | bytes 100
Sparse Core Ops, SparseCore 0:
  8.9 94.8 all-gather.1
where the time goes:
time: 118 us; the launch traced here: 117 us
  blocking collectives  44.8 us (38%)
  waiting for transfers between devices  27.3 us (23%)
  between operations  13.5 us (11%)
  matrix products  10.6 us (9%)
  other arithmetic  9.25 us (8%)
  local copies, waits for them, and re-layouts  6.21 us (5%)
  loops' own time  5.56 us (5%)
    all_gather x1, waiting for transfers between devices, shards(): lax.all_gather(out_weight, 'ctx', axis=1, tiled=True)  26.6 us
    all_gather x1, blocking collectives, shards(): value_piece = lax.all_gather(value_vectors, 'ctx', axis=0, tiled=True)  22.6 us
    all_gather x1, blocking collectives, shards(): key_piece = lax.all_gather(key_vectors, 'ctx', axis=0, tiled=True)  22.3 us
    dot_general x1, matrix products, shards(): jnp.dot(attended, lax.all_gather(out_weight, 'ctx', axis=1, tiled=True),...  6.57 us
    another operation x1, loops' own time, shards(): lax.fori_loop(0, piece_rows // block_rows, one_block, initial)  5.42 us
    dynamic_slice x4, local copies, waits for them, and re-layouts, one_block(): key_block = lax.dynamic_slice_in_dim(key_piece, offset, block_rows, 0)  3.96 us
    reduce_or x4, other arithmetic, one_block(): results.append(lax.cond(jnp.any(sub_mask), compute, keep_state, sub_state))  3.53 us
    dot_general x3, matrix products, update(): jnp.einsum('grk,kd->rgd', probs, value_block, preferred_element_type=jnp....  2.59 us
  transfers between devices with their start and end apart: 1, of which 1 were waited for; matrix products, arithmetic and copies ran while one was open for 17% of the time, Pallas kernels for 0%

commit v1 on v0

--- a/solution.py
+++ b/solution.py
@@ -53,8 +53,13 @@
         jnp.zeros((head_count, span_rows), jnp.float32),
         jnp.zeros((span_rows, head_count, head_width), jnp.float32),
     )
-    key_piece = lax.all_gather(key_vectors, "ctx", axis=0, tiled=True)
-    value_piece = lax.all_gather(value_vectors, "ctx", axis=0, tiled=True)
+    key_piece, value_piece = jnp.split(
+        lax.all_gather(
+            jnp.concatenate([key_vectors, value_vectors], axis=1), "ctx", axis=0, tiled=True
+        ),
+        [key_vectors.shape[1]],
+        axis=1,
+    )
     piece_rows = key_piece.shape[0]
     block_rows = math.gcd(piece_rows, span_rows)
 

time: 118 us -> 135 us (1.14)
  waiting for transfers between devices: 27.3 us -> 86.9 us
  blocking collectives: 44.8 us -> 0 us
  other arithmetic: 9.25 us -> 10.9 us
    all_gather x2 -> x0, blocking collectives: 44.8 us -> none  [the longest x1 22.6 us: shards(): value_piece = lax.all_gather(value_vectors, 'ctx', axis=0, tiled=True)]
    all_gather x1, waiting for transfers between devices: 26.6 us -> 57.8 us  [shards(): lax.all_gather(out_weight, 'ctx', axis=1, tiled=True)]
    all_gather x0 -> x1, waiting for transfers between devices: none -> 28.4 us  [shards(): lax.all_gather(jnp.concatenate([key_vectors, value_vectors], axis=1), 'ct...]
    split x0 -> x1, local copies, waits for them, and re-layouts: none -> 2.25 us  [shards(): jnp.split(lax.all_gather(jnp.concatenate([key_vectors, value_vectors], ax...]
    concatenate x0 -> x1, other arithmetic: none -> 1.76 us  [shards(): jnp.concatenate([key_vectors, value_vectors], axis=1)]
  transfers between devices with their start and end apart: 1 -> 2, of which waited for: 1 -> 2; matrix products, arithmetic and copies ran while one was open for 17% -> 15% of each run, Pallas kernels for 0% -> 0%
where the time goes in v1:
time: 135 us
  waiting for transfers between devices  86.9 us (64%)
  between operations  13.5 us (10%)
  other arithmetic  10.9 us (8%)
  matrix products  10.6 us (8%)
  local copies, waits for them, and re-layouts  7.4 us (5%)
  loops' own time  5.4 us (4%)
    all_gather x1, waiting for transfers between devices, shards(): lax.all_gather(out_weight, 'ctx', axis=1, tiled=True)  57.8 us
    all_gather x1, waiting for transfers between devices, shards(): lax.all_gather(jnp.concatenate([key_vectors, value_vectors], axis=1), 'ct...  28.4 us
    dot_general x1, matrix products, shards(): jnp.dot(attended, lax.all_gather(out_weight, 'ctx', axis=1, tiled=True),...  6.57 us
    another operation x1, loops' own time, shards(): lax.fori_loop(0, piece_rows // block_rows, one_block, initial)  5.26 us
    dynamic_slice x4, local copies, waits for them, and re-layouts, one_block(): key_block = lax.dynamic_slice_in_dim(key_piece, offset, block_rows, 0)  3.95 us
    reduce_or x4, other arithmetic, one_block(): results.append(lax.cond(jnp.any(sub_mask), compute, keep_state, sub_state))  3.4 us
  transfers between devices with their start and end apart: 2, of which 2 were waited for; matrix products, arithmetic and copies ran while one was open for 15% of the time, Pallas kernels for 0%

profile of v1, /device:TPU:0, one launch (start us, length us, event | category | flops | bytes accessed | tf_op | source)
XLA Modules:
  0.0 134.8 jit_solution(15466205037087640618)
XLA Ops:
  6.5 1.8 %pad_maximum_fusion.3 = bf16[512,256]{1,0:T(8,128)(2,1)} fusion(bf16[512,128]{1,0:T(8,128)(2,1)} %param.14, bf16[512,128]{1,0:T(8,128)(2,1)} %param.13), kind=kLoop, calls=%fused_computation.66 | loop fusion | flops 524288 | bytes 524288 | tf_op jit(solution)/shard_map/concatenate | solution.py:58
  8.4 0.7 all-gather.5.cloned.1.call-update
  9.1 0.7 select_reduce_fusion.1
  9.9 0.8 reduce-window.8
  11.3 28.4 %all-gather.3.cloned.1.call-done = bf16[2048,256]{1,0:T(8,128)(2,1)} async-done(((bf16[512,256]{1,0:T(8,128)(2,1)}), bf16[2048,256]{1,0:T(8,128)(2,1)}) %all-gather.3.cloned.1.call-update) | async-done | bytes 1048592 | tf_op jit(solution)/shard_map/all_gather | solution.py:57
  39.6 2.2 %fusion.45 = (bf16[2048,128]{1,0:T(8,128)(2,1)}, bf16[2048,128]{1,0:T(8,128)(2,1)}) fusion(bf16[2048,256]{1,0:T(8,128)(2,1)} %all-gather.3.cloned.1.call-done), kind=kLoop, calls=%fused_computation.84 | loop fusion | bytes 2097152 | tf_op jit(solution)/shard_map/split | solution.py:56
  42.0 21.0 %while.19 = (s32[]{:T(128)}, f32[4,512]{1,0:T(4,128)S(1)}, f32[4,512]{1,0:T(4,128)S(1)}, f32[512,4,128]{2,0,1:T(8,128)S(1)}, s32[8]{0:T(128)S(1)}, /*index=5*/s3...) while((s32[]{:T(128)}, f32[4,512]{1,0:T(4,128)S(1)}, ...), condition=%wide.region_16.17_spmd, body=%wide.region_3.16_spmd.sunk | while | flops 552386560 | bytes 22239732 | solution.py:96
  42.2 0.3 compare_and_fusion.2
  42.5 0.8 slice_reduce_fusion.3
  43.3 1.0 constant_dynamic-slice_fusion.3
  45.0 2.0 %conditional.5 = ((f32[4,256]{1,0:T(4,128)S(1)}, f32[4,256]{1,0:T(4,128)S(1)}, f32[256,4,128]{2,0,1:T(8,128)S(1)})) conditional(s32[]{:T(128)} %convert_element_type.65, (f32[4,256]{1,0:T(4,128)S(1)}, f32[4,256]{1,0:T(4,128)S(1)}, f32[256,4,128]{2,0,1:T(8,128)S(1)}) %tuple.80, (pred[256,512]{0,1:T(8,128)(4,1)S(1)}, ...), branch_computations={%region_7.7_spmd, %region_8.10_spmd} | conditional | flops 275516416 | bytes 8323104 | solution.py:89
  45.1 0.5 fusion
  45.6 0.9 fusion.3
  46.4 0.5 fusion.2
  47.6 1.9 %conditional.4 = ((f32[4,256]{1,0:T(4,128)S(1)}, f32[4,256]{1,0:T(4,128)S(1)}, f32[256,4,128]{2,0,1:T(8,128)S(1)})) conditional(s32[]{:T(128)} %convert_element_type.64, (f32[4,256]{1,0:T(4,128)S(1)}, f32[4,256]{1,0:T(4,128)S(1)}, f32[256,4,128]{2,0,1:T(8,128)S(1)}) %tuple.78, (pred[256,512]{0,1:T(8,128)(4,1)S(1)}, ...), branch_computations={%region_12.12_spmd, %region_13.15_spmd} | conditional | flops 275516416 | bytes 8323104 | solution.py:89
  47.6 0.5 fusion.17
  48.1 0.9 fusion.20
  49.0 0.5 fusion.19
  49.9 0.3 compare_and_fusion.2
  50.2 0.8 slice_reduce_fusion.3
  51.0 1.0 constant_dynamic-slice_fusion.3
  54.0 0.8 slice_reduce_fusion.3
  54.8 1.0 constant_dynamic-slice_fusion.3
  57.2 2.0 %conditional.4 = ((f32[4,256]{1,0:T(4,128)S(1)}, f32[4,256]{1,0:T(4,128)S(1)}, f32[256,4,128]{2,0,1:T(8,128)S(1)})) conditional(s32[]{:T(128)} %convert_element_type.64, (f32[4,256]{1,0:T(4,128)S(1)}, f32[4,256]{1,0:T(4,128)S(1)}, f32[256,4,128]{2,0,1:T(8,128)S(1)}) %tuple.78, (pred[256,512]{0,1:T(8,128)(4,1)S(1)}, ...), branch_computations={%region_12.12_spmd, %region_13.15_spmd} | conditional | flops 275516416 | bytes 8323104 | solution.py:89
  57.2 0.5 fusion.17
  57.7 0.9 fusion.20
  58.6 0.5 fusion.19
  59.7 0.8 slice_reduce_fusion.3
  60.6 1.0 constant_dynamic-slice_fusion.3
  63.0 0.3 copy.18
  63.5 57.8 %all-gather.5.cloned.1.call-done = bf16[512,4096]{1,0:T(8,128)(2,1)} async-done(((bf16[512,1024]{1,0:T(8,128)(2,1)}), bf16[512,4096]{1,0:T(8,128)(2,1)}) %all-gather.5.cloned.1.call-update) | async-done | bytes 4194320 | tf_op jit(solution)/shard_map/all_gather | solution.py:104
  121.4 6.6 %convolution_convert_fusion = bf16[512,4096]{1,0:T(8,128)(2,1)} fusion(bf16[512,512]{0,1:T(8,128)(2,1)S(1)} %bitcast.57, bf16[512,4096]{1,0:T(8,128)(2,1)} %all-gather.5.cloned.1.call-done), kind=kOutput, calls=%fused_computation.64 | convolution fusion | flops 2149580800 | bytes 8912896 | tf_op jit(solution)/shard_map/dot_general | solution.py:102
  (68 shorter events, 3.0 us)
Async XLA Ops:
  6.5 4.1 %copy-start = (bf16[512,512]{1,0:T(8,128)(2,1)S(1)}, bf16[512,512]{1,0:T(8,128)(2,1)}, u32[]{:S(2)}) copy-start(bf16[512,512]{1,0:T(8,128)(2,1)} %param.12) | copy-start | bytes 1572868
  6.5 33.1 %all-gather.3.cloned.1.call-start = ((), (), s32[]{:S(2)}) async-start(), calls=%async_computation | async-start | bytes 1310720 | tf_op jit(solution)/shard_map/all_gather | solution.py:57
  8.3 113.0 %all-gather.5.cloned.1.call-start = ((), (), s32[]{:S(2)}) async-start(), calls=%async_computation.1 | async-start | bytes 5242880 | tf_op jit(solution)/shard_map/all_gather | solution.py:104
  10.9 31.1 %copy-start.1 = (s32[8]{0:T(128)S(1)}, s32[8]{0:T(128)}, u32[]{:S(2)}) copy-start(s32[8]{0:T(128)} %param.15) | copy-start | bytes 100
Sparse Core Ops, SparseCore 0:
  8.9 30.6 all-gather.2
  41.2 80.1 all-gather.4
